TPU v7x, 32 devices: a whole 2x2x4 slice. The times are simulated.
32 devices in a mesh: lat: 4 (over x, core), lon: 8 (over z, y).
Axes of the slice: x: 2, y: 2, z: 4, core: 2. Of those that a mesh axis runs over, the one named last changes fastest.
Arguments:
- queries: bfloat16 [8192, 2048], P(('lat', 'lon')), may hold values from -340 to 340
- keys: bfloat16 [8192, 2048], P(('lat', 'lon')), may hold values from -12 to 12
- values: bfloat16 [8192, 2048], P(('lat', 'lon')), may hold values from -6 to 6
- partners: int32 [32, 5], P(('lat', 'lon')), may hold values from -1 to 31, as said below
- out_weight: bfloat16 [2048, 2048], P(None, 'lat'), may hold values from -0.125 to 0.125
Outputs:
- projected: bfloat16 [8192, 2048], P(('lat', 'lon'))
Inputs may be any that keep to these rules, and one draw needn't show every extreme that they name: `partners`: for each block, the first entries of its row are distinct blocks of its own band, none in its own sector or the two sectors beside it; the remaining entries are -1. In every band some block uses all 5 slots.
All inputs are finite; a program needn't handle non-finite values.
Results may differ from a plain program's by a relative error of at most 0.0095.
Values may be sent and summed in bfloat16 or wider, within the bound.
No kernel may reach another device: no remote copies, remote signals or barrier semaphores. Data moves between devices by JAX's collectives and lax.ppermute only.
A program may use at most 128 MiB of HBM per device.

v0:
```python
import math
import jax
import jax.numpy as jnp
from jax import lax
from jax.sharding import PartitionSpec as P

HEADS = 16
HEAD_DIM = 128
very_low = -1e30


def membership(listed_row, sector, band_start, sectors, lon_count):
    nearby = (
        (sectors == sector)
        | (sectors == (sector + 1) % lon_count)
        | (sectors == (sector + lon_count - 1) % lon_count)
    )
    named = jnp.any(listed_row[:, None] - band_start == sectors[None, :], axis=0)
    return nearby | named


def per_device(queries, keys, values, partners, out_weight):
    lon_count = lax.axis_size("lon")
    band_start = lax.axis_index("lat") * lon_count
    score_scale = 1.0 / math.sqrt(HEAD_DIM)
    sectors = jnp.arange(lon_count, dtype=jnp.int32)
    block_rows = queries.shape[0]
    local_heads = HEADS // lon_count
    q_all, k_all, v_all = (
        lax.all_to_all(queries[None], "lon", split_axis=2, concat_axis=0, tiled=True),
        lax.all_to_all(keys[None], "lon", split_axis=2, concat_axis=0, tiled=True),
        lax.all_to_all(values[None], "lon", split_axis=2, concat_axis=0, tiled=True),
    )
    all_lists = lax.all_gather(partners, "lon", axis=0, tiled=True)
    key_flat = k_all.reshape(lon_count * block_rows, local_heads, HEAD_DIM)
    value_flat = v_all.reshape(lon_count * block_rows, local_heads, HEAD_DIM)

    def one_query(element):
        query_block, listed_row, position = element
        member = membership(listed_row, position, band_start, sectors, lon_count)
        key_mask = jnp.repeat(member, block_rows, total_repeat_length=lon_count * block_rows)
        query_heads = query_block.reshape(block_rows, local_heads, HEAD_DIM)
        scores = (
            jnp.einsum("qhd,khd->hqk", query_heads, key_flat, preferred_element_type=jnp.float32)
            * score_scale
        )
        scores = jnp.where(key_mask[None, None, :], scores, very_low)
        row_max = jnp.max(scores, axis=-1, keepdims=True)
        weights = jnp.exp(scores - row_max)
        row_total = jnp.sum(weights, axis=-1)
        mixture = jnp.einsum(
            "hqk,khd->qhd",
            weights.astype(jnp.bfloat16),
            value_flat,
            preferred_element_type=jnp.float32,
        )
        attended_heads = mixture / row_total.T[:, :, None]
        return attended_heads.reshape(block_rows, local_heads * HEAD_DIM).astype(jnp.bfloat16)

    per_block = lax.map(one_query, (q_all, all_lists, sectors))
    returned = lax.all_to_all(per_block, "lon", split_axis=0, concat_axis=2, tiled=True)
    attended = returned[0]
    projected = jnp.dot(
        attended,
        lax.all_gather(out_weight, "lat", axis=1, tiled=True),
        preferred_element_type=jnp.float32,
    )
    return projected.astype(jnp.bfloat16)


def solution(mesh):
    return jax.shard_map(
        per_device,
        mesh=mesh,
        in_specs=(
            P(("lat", "lon"), None),
            P(("lat", "lon"), None),
            P(("lat", "lon"), None),
            P(("lat", "lon"), None),
            P(None, "lat"),
        ),
        out_specs=P(("lat", "lon"), None),
        check_vma=False,
    )
```

profile of v0, /device:TPU:0, one launch (start us, length us, event | category | flops | bytes accessed | tf_op | source)
XLA Modules:
  0.0 282.5 jit_solution(2650263605104640194)
XLA Ops:
  6.5 4.6 %copy.34 = bf16[1,256,2048]{1,0,2:T(2,128)(2,1)S(1)} copy(bf16[1,256,2048]{2,1,0:T(8,128)(2,1)} %bitcast.106) | data formatting | bytes 2097152 | tf_op jit(solution)/shard_map/broadcast_in_dim | solution.py:31
  11.7 10.6 %reduce.3 = bf16[2048,256]{1,0:T(8,128)(2,1)S(1)} reduce(bf16[2048,1,256]{2,1,0:T(2,128)(2,1)S(1)} %bitcast.98, bf16[]{:T(256)} %broadcast.279), dimensions={1}, to_apply=%bitcast.51.reduce_sub_computation | reduce | bytes 2097154
  22.3 1.1 reshape.254
  23.4 7.3 %all-to-all-start.1 = ((bf16[8,2,32768]{2,1,0:T(2,128)(2,1)}), bf16[8,2,32768]{2,1,0:T(2,128)(2,1)S(1)}, u32[]{:S(2)}, u32[]{:S(2)}) async-start(bf16[8,2,32768]{2,1,0:T(2,128)(2,1)} %reshape.254), calls=%async_computation.1 | async-start | bytes 2097152 | tf_op jit(solution)/shard_map/all_to_all | solution.py:31
  30.7 4.6 %copy.36 = bf16[1,256,2048]{1,0,2:T(2,128)(2,1)S(1)} copy(bf16[1,256,2048]{2,1,0:T(8,128)(2,1)} %bitcast.107) | data formatting | bytes 2097152 | tf_op jit(solution)/shard_map/broadcast_in_dim | solution.py:32
  35.3 11.6 %reduce.4 = bf16[2048,256]{1,0:T(8,128)(2,1)} reduce(bf16[2048,1,256]{2,1,0:T(2,128)(2,1)S(1)} %bitcast.100, bf16[]{:T(256)} %broadcast.279), dimensions={1}, to_apply=%bitcast.53.reduce_sub_computation | reduce | bytes 2097154
  46.9 2.1 reshape.256
  49.0 7.4 %all-to-all-done.1 = bf16[8,2,32768]{2,1,0:T(2,128)(2,1)S(1)} async-done(((bf16[8,2,32768]{2,1,0:T(2,128)(2,1)}), bf16[8,2,32768]{2,1,0:T(2,128)(2,1)S(1)}, u32[]{:S(2)}, u32[]{:S(2)}) %all-to-all-start.1) | async-done | bytes 1048608 | tf_op jit(solution)/shard_map/all_to_all | solution.py:31
  56.5 4.2 %all-to-all-start.2 = ((bf16[8,2,32768]{2,1,0:T(2,128)(2,1)}), bf16[8,2,32768]{2,1,0:T(2,128)(2,1)}, u32[]{:S(2)}, u32[]{:S(2)}) async-start(bf16[8,2,32768]{2,1,0:T(2,128)(2,1)} %reshape.256), calls=%async_computation.2 | async-start | bytes 2097152 | tf_op jit(solution)/shard_map/all_to_all | solution.py:32
  60.7 4.6 %copy.33 = bf16[1,256,2048]{1,0,2:T(2,128)(2,1)S(1)} copy(bf16[1,256,2048]{2,1,0:T(8,128)(2,1)} %bitcast.108) | data formatting | bytes 2097152 | tf_op jit(solution)/shard_map/broadcast_in_dim | solution.py:30
  65.3 11.6 %reduce.2 = bf16[2048,256]{1,0:T(8,128)(2,1)} reduce(bf16[2048,1,256]{2,1,0:T(2,128)(2,1)S(1)} %bitcast.99, bf16[]{:T(256)} %broadcast.279), dimensions={1}, to_apply=%bitcast.49.reduce_sub_computation | reduce | bytes 2097154
  76.9 2.1 reshape.252
  79.0 7.3 %all-to-all-done.2 = bf16[8,2,32768]{2,1,0:T(2,128)(2,1)} async-done(((bf16[8,2,32768]{2,1,0:T(2,128)(2,1)}), bf16[8,2,32768]{2,1,0:T(2,128)(2,1)}, u32[]{:S(2)}, u32[]{:S(2)}) %all-to-all-start.2) | async-done | bytes 1048608 | tf_op jit(solution)/shard_map/all_to_all | solution.py:32
  86.3 4.2 %all-to-all-start = ((bf16[8,2,32768]{2,1,0:T(2,128)(2,1)}), bf16[8,2,32768]{2,1,0:T(2,128)(2,1)}, u32[]{:S(2)}, u32[]{:S(2)}) async-start(bf16[8,2,32768]{2,1,0:T(2,128)(2,1)} %reshape.252), calls=%async_computation | async-start | bytes 2097152 | tf_op jit(solution)/shard_map/all_to_all | solution.py:30
  91.3 30.1 %all-gather = s32[8,1,5]{2,1,0:T(1,128)S(1)} all-gather(s32[1,1,5]{2,1,0:T(1,128)S(1)} %bitcast.111), channel_id=1, replica_groups=mesh['lat'=4,'lon'=8] {'lon'}, dimensions={0}, use_global_device_ids=true | all-gather | bytes 180 | tf_op jit(solution)/shard_map/all_gather | solution.py:34
  121.4 1.0 reshape.255
  124.5 4.3 %reshape.257 = bf16[2048,1,256]{2,1,0:T(2,128)(2,1)S(1)} reshape(bf16[8,2,32768]{2,1,0:T(2,128)(2,1)} %all-to-all-done.2) | data formatting | bytes 2097152
  129.6 1.4 reshape.233
  131.0 4.3 %reshape.253 = bf16[2048,1,256]{2,1,0:T(2,128)(2,1)S(1)} reshape(bf16[8,2,32768]{2,1,0:T(2,128)(2,1)} %all-to-all-done) | data formatting | bytes 2097152
  135.3 1.1 copy.40
  136.5 102.6 %while.18 = (s32[]{:T(128)}, bf16[8,256,256]{1,2,0:T(8,128)(2,1)}, s32[8]{0:T(128)S(1)}, s32[8,5]{1,0:T(8,128)S(1)}, s32[]{:T(128)}, /*index=5*/bf16[8,256,256]{...) while((s32[]{:T(128)}, bf16[8,256,256]{1,2,0:T(8,128)(2,1)}, ...), condition=%wide.region_4.5_spmd.clone, body=%wide.region_0.4_spmd.clone.sunk | while | flops 548549760 | bytes 19694732 | solution.py:60
  139.9 4.9 %select_select_fusion.2 = pred[2048]{0:T(1024)(128)(4,1)S(1)} fusion(pred[2048]{0:T(1024)(128)(4,1)S(1)} %get-tuple-element.493, pred[2048]{0:T(1024)(128)(4,1)S(1)} %get-tuple-element.494, pred[2048]{0:T(1024)(128)(4,1)S(1)} %get-tuple-element.495, pred[2048]{0:T(1024)(128)(4,1)S(1)} %get-tuple-element.496, ...), kind=kLoop, calls=%fused_computation.10.clone.1 | loop fusion | flops 14336 | bytes 16392 | tf_op jit(solution)/shard_map/while/body/eval_jaxpr/jit(_take)/gather | solution.py:41
  146.6 0.9 fusion.41
  147.5 1.1 fusion.42
  152.7 4.9 %select_select_fusion.2 = pred[2048]{0:T(1024)(128)(4,1)S(1)} fusion(pred[2048]{0:T(1024)(128)(4,1)S(1)} %get-tuple-element.493, pred[2048]{0:T(1024)(128)(4,1)S(1)} %get-tuple-element.494, pred[2048]{0:T(1024)(128)(4,1)S(1)} %get-tuple-element.495, pred[2048]{0:T(1024)(128)(4,1)S(1)} %get-tuple-element.496, ...), kind=kLoop, calls=%fused_computation.10.clone.1 | loop fusion | flops 14336 | bytes 16392 | tf_op jit(solution)/shard_map/while/body/eval_jaxpr/jit(_take)/gather | solution.py:41
  158.5 0.9 fusion.40
  159.4 0.9 fusion.41
  160.4 1.1 fusion.42
  165.5 4.9 %select_select_fusion.2 = pred[2048]{0:T(1024)(128)(4,1)S(1)} fusion(pred[2048]{0:T(1024)(128)(4,1)S(1)} %get-tuple-element.493, pred[2048]{0:T(1024)(128)(4,1)S(1)} %get-tuple-element.494, pred[2048]{0:T(1024)(128)(4,1)S(1)} %get-tuple-element.495, pred[2048]{0:T(1024)(128)(4,1)S(1)} %get-tuple-element.496, ...), kind=kLoop, calls=%fused_computation.10.clone.1 | loop fusion | flops 14336 | bytes 16392 | tf_op jit(solution)/shard_map/while/body/eval_jaxpr/jit(_take)/gather | solution.py:41
  172.2 0.9 fusion.41
  173.2 1.1 fusion.42
  178.3 4.9 %select_select_fusion.2 = pred[2048]{0:T(1024)(128)(4,1)S(1)} fusion(pred[2048]{0:T(1024)(128)(4,1)S(1)} %get-tuple-element.493, pred[2048]{0:T(1024)(128)(4,1)S(1)} %get-tuple-element.494, pred[2048]{0:T(1024)(128)(4,1)S(1)} %get-tuple-element.495, pred[2048]{0:T(1024)(128)(4,1)S(1)} %get-tuple-element.496, ...), kind=kLoop, calls=%fused_computation.10.clone.1 | loop fusion | flops 14336 | bytes 16392 | tf_op jit(solution)/shard_map/while/body/eval_jaxpr/jit(_take)/gather | solution.py:41
  185.0 0.9 fusion.41
  186.0 1.1 fusion.42
  191.1 4.9 %select_select_fusion.2 = pred[2048]{0:T(1024)(128)(4,1)S(1)} fusion(pred[2048]{0:T(1024)(128)(4,1)S(1)} %get-tuple-element.493, pred[2048]{0:T(1024)(128)(4,1)S(1)} %get-tuple-element.494, pred[2048]{0:T(1024)(128)(4,1)S(1)} %get-tuple-element.495, pred[2048]{0:T(1024)(128)(4,1)S(1)} %get-tuple-element.496, ...), kind=kLoop, calls=%fused_computation.10.clone.1 | loop fusion | flops 14336 | bytes 16392 | tf_op jit(solution)/shard_map/while/body/eval_jaxpr/jit(_take)/gather | solution.py:41
  197.9 0.9 fusion.41
  198.8 1.1 fusion.42
  204.0 4.9 %select_select_fusion.2 = pred[2048]{0:T(1024)(128)(4,1)S(1)} fusion(pred[2048]{0:T(1024)(128)(4,1)S(1)} %get-tuple-element.493, pred[2048]{0:T(1024)(128)(4,1)S(1)} %get-tuple-element.494, pred[2048]{0:T(1024)(128)(4,1)S(1)} %get-tuple-element.495, pred[2048]{0:T(1024)(128)(4,1)S(1)} %get-tuple-element.496, ...), kind=kLoop, calls=%fused_computation.10.clone.1 | loop fusion | flops 14336 | bytes 16392 | tf_op jit(solution)/shard_map/while/body/eval_jaxpr/jit(_take)/gather | solution.py:41
  210.7 0.9 fusion.41
  211.6 1.1 fusion.42
  216.8 4.9 %select_select_fusion.2 = pred[2048]{0:T(1024)(128)(4,1)S(1)} fusion(pred[2048]{0:T(1024)(128)(4,1)S(1)} %get-tuple-element.493, pred[2048]{0:T(1024)(128)(4,1)S(1)} %get-tuple-element.494, pred[2048]{0:T(1024)(128)(4,1)S(1)} %get-tuple-element.495, pred[2048]{0:T(1024)(128)(4,1)S(1)} %get-tuple-element.496, ...), kind=kLoop, calls=%fused_computation.10.clone.1 | loop fusion | flops 14336 | bytes 16392 | tf_op jit(solution)/shard_map/while/body/eval_jaxpr/jit(_take)/gather | solution.py:41
  223.5 0.9 fusion.41
  224.5 1.1 fusion.42
  229.6 4.9 %select_select_fusion.2 = pred[2048]{0:T(1024)(128)(4,1)S(1)} fusion(pred[2048]{0:T(1024)(128)(4,1)S(1)} %get-tuple-element.493, pred[2048]{0:T(1024)(128)(4,1)S(1)} %get-tuple-element.494, pred[2048]{0:T(1024)(128)(4,1)S(1)} %get-tuple-element.495, pred[2048]{0:T(1024)(128)(4,1)S(1)} %get-tuple-element.496, ...), kind=kLoop, calls=%fused_computation.10.clone.1 | loop fusion | flops 14336 | bytes 16392 | tf_op jit(solution)/shard_map/while/body/eval_jaxpr/jit(_take)/gather | solution.py:41
  236.3 0.9 fusion.41
  237.3 1.1 fusion.42
  239.1 29.9 %all_to_all.63 = bf16[8,256,256]{1,2,0:T(8,128)(2,1)S(1)} all-to-all(bf16[8,256,256]{1,2,0:T(8,128)(2,1)} %get-tuple-element.287), channel_id=1, replica_groups=mesh['lat'=4,'lon'=8] {'lon'}, dimensions={0} | all-to-all | bytes 2097152 | tf_op jit(solution)/shard_map/all_to_all | solution.py:61
  269.0 6.7 %convolution_convert_fusion = bf16[256,2048]{1,0:T(8,128)(2,1)} fusion(bf16[256,2048]{0,1:T(8,128)(2,1)S(1)} %bitcast.101, bf16[2048,2048]{1,0:T(8,128)(2,1)} %all-gather.3.cloned.1.call-done), kind=kOutput, calls=%fused_computation.20 | convolution fusion | flops 2148007936 | bytes 10485760 | tf_op jit(solution)/shard_map/dot_general | solution.py:63
  (108 shorter events, 39.5 us)
Async XLA Ops:
  23.4 33.1 %all-to-all-start.1 = ((bf16[8,2,32768]{2,1,0:T(2,128)(2,1)}), bf16[8,2,32768]{2,1,0:T(2,128)(2,1)S(1)}, u32[]{:S(2)}, u32[]{:S(2)}) async-start(bf16[8,2,32768]{2,1,0:T(2,128)(2,1)} %reshape.254), calls=%async_computation.1 | async-start | bytes 2097152 | tf_op jit(solution)/shard_map/all_to_all | solution.py:31
  56.5 29.8 %all-to-all-start.2 = ((bf16[8,2,32768]{2,1,0:T(2,128)(2,1)}), bf16[8,2,32768]{2,1,0:T(2,128)(2,1)}, u32[]{:S(2)}, u32[]{:S(2)}) async-start(bf16[8,2,32768]{2,1,0:T(2,128)(2,1)} %reshape.256), calls=%async_computation.2 | async-start | bytes 2097152 | tf_op jit(solution)/shard_map/all_to_all | solution.py:32
  65.3 26.0 %copy-start.8 = (s32[1,5]{1,0:T(1,128)S(1)}, s32[1,5]{1,0:T(1,128)}, u32[]{:S(2)}) copy-start(s32[1,5]{1,0:T(1,128)} %param.12) | copy-start | bytes 64
  86.3 44.7 %all-to-all-start = ((bf16[8,2,32768]{2,1,0:T(2,128)(2,1)}), bf16[8,2,32768]{2,1,0:T(2,128)(2,1)}, u32[]{:S(2)}, u32[]{:S(2)}) async-start(bf16[8,2,32768]{2,1,0:T(2,128)(2,1)} %reshape.252), calls=%async_computation | async-start | bytes 2097152 | tf_op jit(solution)/shard_map/all_to_all | solution.py:30
  90.5 178.4 %all-gather.3.cloned.1.call-start = ((), (), s32[]{:S(2)}) async-start(), calls=%async_computation.4 | async-start | bytes 10485760 | tf_op jit(solution)/shard_map/all_gather | solution.py:65
  129.6 6.9 %copy-start.1 = (pred[2048]{0:T(1024)(128)(4,1)S(1)}, pred[2048]{0:T(1024)(128)(4,1)}, u32[]{:S(2)}) copy-start(pred[2048]{0:T(1024)(128)(4,1)} %constant.324) | copy-start | bytes 6148
  129.6 6.9 %copy-start.2 = (pred[2048]{0:T(1024)(128)(4,1)S(1)}, pred[2048]{0:T(1024)(128)(4,1)}, u32[]{:S(2)}) copy-start(pred[2048]{0:T(1024)(128)(4,1)} %constant.325) | copy-start | bytes 6148
  129.6 6.9 %copy-start.3 = (pred[2048]{0:T(1024)(128)(4,1)S(1)}, pred[2048]{0:T(1024)(128)(4,1)}, u32[]{:S(2)}) copy-start(pred[2048]{0:T(1024)(128)(4,1)} %constant.326) | copy-start | bytes 6148
  129.6 6.9 %copy-start.4 = (pred[2048]{0:T(1024)(128)(4,1)S(1)}, pred[2048]{0:T(1024)(128)(4,1)}, u32[]{:S(2)}) copy-start(pred[2048]{0:T(1024)(128)(4,1)} %constant.327) | copy-start | bytes 6148
  129.6 6.9 %copy-start.5 = (pred[2048]{0:T(1024)(128)(4,1)S(1)}, pred[2048]{0:T(1024)(128)(4,1)}, u32[]{:S(2)}) copy-start(pred[2048]{0:T(1024)(128)(4,1)} %constant.328) | copy-start | bytes 6148
  129.6 6.9 %copy-start.6 = (pred[2048]{0:T(1024)(128)(4,1)S(1)}, pred[2048]{0:T(1024)(128)(4,1)}, u32[]{:S(2)}) copy-start(pred[2048]{0:T(1024)(128)(4,1)} %constant.329) | copy-start | bytes 6148
  129.6 6.9 %copy-start.7 = (pred[2048]{0:T(1024)(128)(4,1)S(1)}, pred[2048]{0:T(1024)(128)(4,1)}, u32[]{:S(2)}) copy-start(pred[2048]{0:T(1024)(128)(4,1)} %constant.330) | copy-start | bytes 6148
  145.7 1.9 copy-start
  158.5 1.9 copy-start
  171.3 1.9 copy-start
  184.1 1.9 copy-start
  196.9 1.9 copy-start
  209.8 1.9 copy-start
  222.6 1.9 copy-start
  235.4 1.9 copy-start
Sparse Core Ops, SparseCore 0:
  92.9 59.5 all-gather.2
where the time goes:
time: 284 us; the launch traced here: 283 us
  other arithmetic  86.1 us (30%)
  blocking collectives  60 us (21%)
  local copies, waits for them, and re-layouts  57.7 us (20%)
  matrix products  23.1 us (8%)
  starting transfers between devices  15.8 us (6%)
  waiting for transfers between devices  15.4 us (5%)
  between operations  13.6 us (5%)
  loops' own time  10.8 us (4%)
    gather x8, other arithmetic, one_query(): jnp.repeat(member, block_rows, total_repeat_length=lon_count * block_rows)  38.9 us
    unnamed x3, other arithmetic  33.7 us
    all_gather x1, blocking collectives, per_device(): all_lists = lax.all_gather(partners, 'lon', axis=0, tiled=True)  30.1 us
    all_to_all x1, blocking collectives, per_device(): lax.all_to_all(per_block, 'lon', split_axis=0, concat_axis=2, tiled=True)  29.9 us
    unnamed x27, local copies, waits for them, and re-layouts  17.8 us
    dynamic_slice x16, local copies, waits for them, and re-layouts, per_device(): per_block = lax.map(one_query, (q_all, all_lists, sectors))  12.2 us
    another operation x1, loops' own time, per_device(): per_block = lax.map(one_query, (q_all, all_lists, sectors))  10.8 us
    dot_general x8, matrix products, one_query(): jnp.einsum('hqk,khd->qhd', weights.astype(jnp.bfloat16), value_flat, pref...  9.01 us
  transfers between devices with their start and end apart: 4, of which 2 were waited for; matrix products, arithmetic and copies ran while one was open for 51% of the time, Pallas kernels for 0%

commit v1 on v0

--- a/solution.py
+++ b/solution.py
@@ -31,7 +31,12 @@
         lax.all_to_all(keys[None], "lon", split_axis=2, concat_axis=0, tiled=True),
         lax.all_to_all(values[None], "lon", split_axis=2, concat_axis=0, tiled=True),
     )
-    all_lists = lax.all_gather(partners, "lon", axis=0, tiled=True)
+    ring = [partners]
+    for hop in range(7):
+        ring.append(lax.ppermute(ring[-1], "lon", [(dev, (dev + 1) % 8) for dev in range(8)]))
+    all_lists = jnp.roll(
+        jnp.concatenate(ring[::-1], axis=0), (lax.axis_index("lon") + 1) * ring[0].shape[0], axis=0
+    )
     key_flat = k_all.reshape(lon_count * block_rows, local_heads, HEAD_DIM)
     value_flat = v_all.reshape(lon_count * block_rows, local_heads, HEAD_DIM)
 

time: 284 us -> 304 us (1.070)
  waiting for transfers between devices: 15.4 us -> 71.5 us
  blocking collectives: 60 us -> 21.1 us
    ppermute x0 -> x7, waiting for transfers between devices: none -> 56.9 us  [per_device(): lax.ppermute(ring[-1], 'lon', [(dev, (dev + 1) % 8) for dev in range(8)])]
    all_gather x1 -> x0, blocking collectives: 30.1 us -> none  [per_device(): all_lists = lax.all_gather(partners, 'lon', axis=0, tiled=True)]
    all_to_all x1, blocking collectives: 29.9 us -> 21.1 us  [per_device(): lax.all_to_all(per_block, 'lon', split_axis=0, concat_axis=2, tiled=True)]
  transfers between devices with their start and end apart: 4 -> 11, of which waited for: 2 -> 9; matrix products, arithmetic and copies ran while one was open for 51% -> 48% of each run, Pallas kernels for 0% -> 0%
where the time goes in v1:
time: 304 us; the launch traced here: 302 us
  other arithmetic  86.7 us (29%)
  waiting for transfers between devices  71.5 us (24%)
  local copies, waits for them, and re-layouts  57.7 us (19%)
  matrix products  23 us (8%)
  blocking collectives  21.1 us (7%)
  starting transfers between devices  17.8 us (6%)
  between operations  13.7 us (5%)
  loops' own time  10.6 us (3%)
    ppermute x7, waiting for transfers between devices, per_device(): lax.ppermute(ring[-1], 'lon', [(dev, (dev + 1) % 8) for dev in range(8)])  56.9 us
    gather x8, other arithmetic, one_query(): jnp.repeat(member, block_rows, total_repeat_length=lon_count * block_rows)  39.4 us
    unnamed x3, other arithmetic  33.9 us
    all_to_all x1, blocking collectives, per_device(): lax.all_to_all(per_block, 'lon', split_axis=0, concat_axis=2, tiled=True)  21.1 us
    unnamed x27, local copies, waits for them, and re-layouts  17.8 us
    dynamic_slice x16, local copies, waits for them, and re-layouts, per_device(): per_block = lax.map(one_query, (q_all, all_lists, sectors))  12.1 us
    another operation x1, loops' own time, per_device(): per_block = lax.map(one_query, (q_all, all_lists, sectors))  10.6 us
    dot_general x8, matrix products, one_query(): jnp.einsum('hqk,khd->qhd', weights.astype(jnp.bfloat16), value_flat, pref...  9.01 us
  transfers between devices with their start and end apart: 11, of which 9 were waited for; matrix products, arithmetic and copies ran while one was open for 48% of the time, Pallas kernels for 0%

profile of v1, /device:TPU:0, one launch (start us, length us, event | category | flops | bytes accessed | tf_op | source)
XLA Modules:
  0.0 302.0 jit_solution(14166030513742195780)
XLA Ops:
  6.5 4.6 %copy.34 = bf16[1,256,2048]{1,0,2:T(2,128)(2,1)S(1)} copy(bf16[1,256,2048]{2,1,0:T(8,128)(2,1)} %bitcast.104) | data formatting | bytes 2097152 | tf_op jit(solution)/shard_map/broadcast_in_dim | solution.py:31
  11.7 10.6 %reduce.3 = bf16[2048,256]{1,0:T(8,128)(2,1)S(1)} reduce(bf16[2048,1,256]{2,1,0:T(2,128)(2,1)S(1)} %bitcast.96, bf16[]{:T(256)} %broadcast.280), dimensions={1}, to_apply=%bitcast.49.reduce_sub_computation | reduce | bytes 2097154
  22.4 1.1 reshape.252
  23.5 7.3 %all-to-all-start.1 = ((bf16[8,2,32768]{2,1,0:T(2,128)(2,1)}), bf16[8,2,32768]{2,1,0:T(2,128)(2,1)S(1)}, u32[]{:S(2)}, u32[]{:S(2)}) async-start(bf16[8,2,32768]{2,1,0:T(2,128)(2,1)} %reshape.252), calls=%async_computation.1 | async-start | bytes 2097152 | tf_op jit(solution)/shard_map/all_to_all | solution.py:31
  30.8 4.6 %copy.36 = bf16[1,256,2048]{1,0,2:T(2,128)(2,1)S(1)} copy(bf16[1,256,2048]{2,1,0:T(8,128)(2,1)} %bitcast.105) | data formatting | bytes 2097152 | tf_op jit(solution)/shard_map/broadcast_in_dim | solution.py:32
  35.4 11.6 %reduce.4 = bf16[2048,256]{1,0:T(8,128)(2,1)} reduce(bf16[2048,1,256]{2,1,0:T(2,128)(2,1)S(1)} %bitcast.98, bf16[]{:T(256)} %broadcast.280), dimensions={1}, to_apply=%bitcast.51.reduce_sub_computation | reduce | bytes 2097154
  47.0 2.1 reshape.254
  49.2 7.4 %all-to-all-done.1 = bf16[8,2,32768]{2,1,0:T(2,128)(2,1)S(1)} async-done(((bf16[8,2,32768]{2,1,0:T(2,128)(2,1)}), bf16[8,2,32768]{2,1,0:T(2,128)(2,1)S(1)}, u32[]{:S(2)}, u32[]{:S(2)}) %all-to-all-start.1) | async-done | bytes 1048608 | tf_op jit(solution)/shard_map/all_to_all | solution.py:31
  56.5 4.3 %all-to-all-start.2 = ((bf16[8,2,32768]{2,1,0:T(2,128)(2,1)}), bf16[8,2,32768]{2,1,0:T(2,128)(2,1)}, u32[]{:S(2)}, u32[]{:S(2)}) async-start(bf16[8,2,32768]{2,1,0:T(2,128)(2,1)} %reshape.254), calls=%async_computation.2 | async-start | bytes 2097152 | tf_op jit(solution)/shard_map/all_to_all | solution.py:32
  60.8 4.6 %copy.33 = bf16[1,256,2048]{1,0,2:T(2,128)(2,1)S(1)} copy(bf16[1,256,2048]{2,1,0:T(8,128)(2,1)} %bitcast.106) | data formatting | bytes 2097152 | tf_op jit(solution)/shard_map/broadcast_in_dim | solution.py:30
  65.4 11.6 %reduce.2 = bf16[2048,256]{1,0:T(8,128)(2,1)} reduce(bf16[2048,1,256]{2,1,0:T(2,128)(2,1)S(1)} %bitcast.97, bf16[]{:T(256)} %broadcast.280), dimensions={1}, to_apply=%bitcast.47.reduce_sub_computation | reduce | bytes 2097154
  77.0 2.1 reshape.250
  79.1 7.2 %all-to-all-done.2 = bf16[8,2,32768]{2,1,0:T(2,128)(2,1)} async-done(((bf16[8,2,32768]{2,1,0:T(2,128)(2,1)}), bf16[8,2,32768]{2,1,0:T(2,128)(2,1)}, u32[]{:S(2)}, u32[]{:S(2)}) %all-to-all-start.2) | async-done | bytes 1048608 | tf_op jit(solution)/shard_map/all_to_all | solution.py:32
  86.4 4.3 %all-to-all-start = ((bf16[8,2,32768]{2,1,0:T(2,128)(2,1)}), bf16[8,2,32768]{2,1,0:T(2,128)(2,1)}, u32[]{:S(2)}, u32[]{:S(2)}) async-start(bf16[8,2,32768]{2,1,0:T(2,128)(2,1)} %reshape.250), calls=%async_computation | async-start | bytes 2097152 | tf_op jit(solution)/shard_map/all_to_all | solution.py:30
  90.7 1.9 collective-permute-start
  92.7 19.4 %collective-permute-done = s32[1,5]{1,0:T(1,128)S(1)} collective-permute-done((s32[1,5]{1,0:T(1,128)S(1)}, s32[1,5]{1,0:T(1,128)S(1)}, u32[]{:S(2)}, u32[]{:S(2)}) %collective-permute-start) | collective-permute-done | bytes 52 | tf_op jit(solution)/shard_map/ppermute | solution.py:36
  112.0 6.3 %collective-permute-done.1 = s32[1,5]{1,0:T(1,128)S(1)} collective-permute-done((s32[1,5]{1,0:T(1,128)S(1)}, s32[1,5]{1,0:T(1,128)S(1)}, u32[]{:S(2)}, u32[]{:S(2)}) %collective-permute-start.1) | collective-permute-done | bytes 52 | tf_op jit(solution)/shard_map/ppermute | solution.py:36
  118.3 6.3 %collective-permute-done.2 = s32[1,5]{1,0:T(1,128)S(1)} collective-permute-done((s32[1,5]{1,0:T(1,128)S(1)}, s32[1,5]{1,0:T(1,128)S(1)}, u32[]{:S(2)}, u32[]{:S(2)}) %collective-permute-start.2) | collective-permute-done | bytes 52 | tf_op jit(solution)/shard_map/ppermute | solution.py:36
  124.5 6.3 %collective-permute-done.3 = s32[1,5]{1,0:T(1,128)S(1)} collective-permute-done((s32[1,5]{1,0:T(1,128)S(1)}, s32[1,5]{1,0:T(1,128)S(1)}, u32[]{:S(2)}, u32[]{:S(2)}) %collective-permute-start.3) | collective-permute-done | bytes 52 | tf_op jit(solution)/shard_map/ppermute | solution.py:36
  130.8 6.3 %collective-permute-done.4 = s32[1,5]{1,0:T(1,128)S(1)} collective-permute-done((s32[1,5]{1,0:T(1,128)S(1)}, s32[1,5]{1,0:T(1,128)S(1)}, u32[]{:S(2)}, u32[]{:S(2)}) %collective-permute-start.4) | collective-permute-done | bytes 52 | tf_op jit(solution)/shard_map/ppermute | solution.py:36
  137.1 6.3 %collective-permute-done.5 = s32[1,5]{1,0:T(1,128)S(1)} collective-permute-done((s32[1,5]{1,0:T(1,128)S(1)}, s32[1,5]{1,0:T(1,128)S(1)}, u32[]{:S(2)}, u32[]{:S(2)}) %collective-permute-start.5) | collective-permute-done | bytes 52 | tf_op jit(solution)/shard_map/ppermute | solution.py:36
  143.3 6.3 %collective-permute-done.6 = s32[1,5]{1,0:T(1,128)S(1)} collective-permute-done((s32[1,5]{1,0:T(1,128)S(1)}, s32[1,5]{1,0:T(1,128)S(1)}, u32[]{:S(2)}, u32[]{:S(2)}) %collective-permute-start.6) | collective-permute-done | bytes 52 | tf_op jit(solution)/shard_map/ppermute | solution.py:36
  149.7 1.1 reshape.253
  152.7 4.3 %reshape.255 = bf16[2048,1,256]{2,1,0:T(2,128)(2,1)S(1)} reshape(bf16[8,2,32768]{2,1,0:T(2,128)(2,1)} %all-to-all-done.2) | data formatting | bytes 2097152
  157.9 1.4 reshape.233
  159.3 4.3 %reshape.251 = bf16[2048,1,256]{2,1,0:T(2,128)(2,1)S(1)} reshape(bf16[8,2,32768]{2,1,0:T(2,128)(2,1)} %all-to-all-done) | data formatting | bytes 2097152
  163.6 1.1 copy.40
  164.8 102.6 %while.18 = (s32[]{:T(128)}, bf16[8,256,256]{1,2,0:T(8,128)(2,1)}, s32[8]{0:T(128)S(1)}, s32[8,5]{1,0:T(8,128)S(1)}, s32[]{:T(128)}, /*index=5*/bf16[8,256,256]{...) while((s32[]{:T(128)}, bf16[8,256,256]{1,2,0:T(8,128)(2,1)}, ...), condition=%wide.region_4.5_spmd.clone, body=%wide.region_0.4_spmd.clone.sunk | while | flops 548549760 | bytes 19694732 | solution.py:65
  168.1 4.9 %select_select_fusion.2 = pred[2048]{0:T(1024)(128)(4,1)S(1)} fusion(pred[2048]{0:T(1024)(128)(4,1)S(1)} %get-tuple-element.493, pred[2048]{0:T(1024)(128)(4,1)S(1)} %get-tuple-element.494, pred[2048]{0:T(1024)(128)(4,1)S(1)} %get-tuple-element.495, pred[2048]{0:T(1024)(128)(4,1)S(1)} %get-tuple-element.496, ...), kind=kLoop, calls=%fused_computation.10.clone.1 | loop fusion | flops 14336 | bytes 16392 | tf_op jit(solution)/shard_map/while/body/eval_jaxpr/jit(_take)/gather | solution.py:46
  175.8 1.1 fusion.42
  180.9 4.9 %select_select_fusion.2 = pred[2048]{0:T(1024)(128)(4,1)S(1)} fusion(pred[2048]{0:T(1024)(128)(4,1)S(1)} %get-tuple-element.493, pred[2048]{0:T(1024)(128)(4,1)S(1)} %get-tuple-element.494, pred[2048]{0:T(1024)(128)(4,1)S(1)} %get-tuple-element.495, pred[2048]{0:T(1024)(128)(4,1)S(1)} %get-tuple-element.496, ...), kind=kLoop, calls=%fused_computation.10.clone.1 | loop fusion | flops 14336 | bytes 16392 | tf_op jit(solution)/shard_map/while/body/eval_jaxpr/jit(_take)/gather | solution.py:46
  187.7 0.9 fusion.41
  188.6 1.1 fusion.42
  193.7 4.9 %select_select_fusion.2 = pred[2048]{0:T(1024)(128)(4,1)S(1)} fusion(pred[2048]{0:T(1024)(128)(4,1)S(1)} %get-tuple-element.493, pred[2048]{0:T(1024)(128)(4,1)S(1)} %get-tuple-element.494, pred[2048]{0:T(1024)(128)(4,1)S(1)} %get-tuple-element.495, pred[2048]{0:T(1024)(128)(4,1)S(1)} %get-tuple-element.496, ...), kind=kLoop, calls=%fused_computation.10.clone.1 | loop fusion | flops 14336 | bytes 16392 | tf_op jit(solution)/shard_map/while/body/eval_jaxpr/jit(_take)/gather | solution.py:46
  200.5 0.9 fusion.41
  201.4 1.1 fusion.42
  206.5 4.9 %select_select_fusion.2 = pred[2048]{0:T(1024)(128)(4,1)S(1)} fusion(pred[2048]{0:T(1024)(128)(4,1)S(1)} %get-tuple-element.493, pred[2048]{0:T(1024)(128)(4,1)S(1)} %get-tuple-element.494, pred[2048]{0:T(1024)(128)(4,1)S(1)} %get-tuple-element.495, pred[2048]{0:T(1024)(128)(4,1)S(1)} %get-tuple-element.496, ...), kind=kLoop, calls=%fused_computation.10.clone.1 | loop fusion | flops 14336 | bytes 16392 | tf_op jit(solution)/shard_map/while/body/eval_jaxpr/jit(_take)/gather | solution.py:46
  214.3 1.1 fusion.42
  219.4 4.9 %select_select_fusion.2 = pred[2048]{0:T(1024)(128)(4,1)S(1)} fusion(pred[2048]{0:T(1024)(128)(4,1)S(1)} %get-tuple-element.493, pred[2048]{0:T(1024)(128)(4,1)S(1)} %get-tuple-element.494, pred[2048]{0:T(1024)(128)(4,1)S(1)} %get-tuple-element.495, pred[2048]{0:T(1024)(128)(4,1)S(1)} %get-tuple-element.496, ...), kind=kLoop, calls=%fused_computation.10.clone.1 | loop fusion | flops 14336 | bytes 16392 | tf_op jit(solution)/shard_map/while/body/eval_jaxpr/jit(_take)/gather | solution.py:46
  227.1 1.1 fusion.42
  232.2 4.9 %select_select_fusion.2 = pred[2048]{0:T(1024)(128)(4,1)S(1)} fusion(pred[2048]{0:T(1024)(128)(4,1)S(1)} %get-tuple-element.493, pred[2048]{0:T(1024)(128)(4,1)S(1)} %get-tuple-element.494, pred[2048]{0:T(1024)(128)(4,1)S(1)} %get-tuple-element.495, pred[2048]{0:T(1024)(128)(4,1)S(1)} %get-tuple-element.496, ...), kind=kLoop, calls=%fused_computation.10.clone.1 | loop fusion | flops 14336 | bytes 16392 | tf_op jit(solution)/shard_map/while/body/eval_jaxpr/jit(_take)/gather | solution.py:46
  239.9 1.1 fusion.42
  245.0 4.9 %select_select_fusion.2 = pred[2048]{0:T(1024)(128)(4,1)S(1)} fusion(pred[2048]{0:T(1024)(128)(4,1)S(1)} %get-tuple-element.493, pred[2048]{0:T(1024)(128)(4,1)S(1)} %get-tuple-element.494, pred[2048]{0:T(1024)(128)(4,1)S(1)} %get-tuple-element.495, pred[2048]{0:T(1024)(128)(4,1)S(1)} %get-tuple-element.496, ...), kind=kLoop, calls=%fused_computation.10.clone.1 | loop fusion | flops 14336 | bytes 16392 | tf_op jit(solution)/shard_map/while/body/eval_jaxpr/jit(_take)/gather | solution.py:46
  252.7 1.1 fusion.42
  257.8 4.9 %select_select_fusion.2 = pred[2048]{0:T(1024)(128)(4,1)S(1)} fusion(pred[2048]{0:T(1024)(128)(4,1)S(1)} %get-tuple-element.493, pred[2048]{0:T(1024)(128)(4,1)S(1)} %get-tuple-element.494, pred[2048]{0:T(1024)(128)(4,1)S(1)} %get-tuple-element.495, pred[2048]{0:T(1024)(128)(4,1)S(1)} %get-tuple-element.496, ...), kind=kLoop, calls=%fused_computation.10.clone.1 | loop fusion | flops 14336 | bytes 16392 | tf_op jit(solution)/shard_map/while/body/eval_jaxpr/jit(_take)/gather | solution.py:46
  265.6 1.1 fusion.42
  267.4 21.1 %all_to_all.63 = bf16[8,256,256]{1,2,0:T(8,128)(2,1)S(1)} all-to-all(bf16[8,256,256]{1,2,0:T(8,128)(2,1)} %get-tuple-element.287), channel_id=1, replica_groups=mesh['lat'=4,'lon'=8] {'lon'}, dimensions={0} | all-to-all | bytes 2097152 | tf_op jit(solution)/shard_map/all_to_all | solution.py:66
  288.5 6.7 %convolution_convert_fusion = bf16[256,2048]{1,0:T(8,128)(2,1)} fusion(bf16[256,2048]{0,1:T(8,128)(2,1)S(1)} %bitcast.99, bf16[2048,2048]{1,0:T(8,128)(2,1)} %all-gather.2.cloned.1.call-done), kind=kOutput, calls=%fused_computation.20 | convolution fusion | flops 2148007936 | bytes 10485760 | tf_op jit(solution)/shard_map/dot_general | solution.py:68
  (123 shorter events, 45.2 us)
Async XLA Ops:
  23.5 33.1 %all-to-all-start.1 = ((bf16[8,2,32768]{2,1,0:T(2,128)(2,1)}), bf16[8,2,32768]{2,1,0:T(2,128)(2,1)S(1)}, u32[]{:S(2)}, u32[]{:S(2)}) async-start(bf16[8,2,32768]{2,1,0:T(2,128)(2,1)} %reshape.252), calls=%async_computation.1 | async-start | bytes 2097152 | tf_op jit(solution)/shard_map/all_to_all | solution.py:31
  56.5 29.8 %all-to-all-start.2 = ((bf16[8,2,32768]{2,1,0:T(2,128)(2,1)}), bf16[8,2,32768]{2,1,0:T(2,128)(2,1)}, u32[]{:S(2)}, u32[]{:S(2)}) async-start(bf16[8,2,32768]{2,1,0:T(2,128)(2,1)} %reshape.254), calls=%async_computation.2 | async-start | bytes 2097152 | tf_op jit(solution)/shard_map/all_to_all | solution.py:32
  65.4 25.3 %copy-start.8 = (s32[1,5]{1,0:T(1,128)S(1)}, s32[1,5]{1,0:T(1,128)}, u32[]{:S(2)}) copy-start(s32[1,5]{1,0:T(1,128)} %param.12) | copy-start | bytes 64
  86.4 72.9 %all-to-all-start = ((bf16[8,2,32768]{2,1,0:T(2,128)(2,1)}), bf16[8,2,32768]{2,1,0:T(2,128)(2,1)}, u32[]{:S(2)}, u32[]{:S(2)}) async-start(bf16[8,2,32768]{2,1,0:T(2,128)(2,1)} %reshape.250), calls=%async_computation | async-start | bytes 2097152 | tf_op jit(solution)/shard_map/all_to_all | solution.py:30
  90.6 197.9 %all-gather.2.cloned.1.call-start = ((), (), s32[]{:S(2)}) async-start(), calls=%async_computation.4 | async-start | bytes 10485760 | tf_op jit(solution)/shard_map/all_gather | solution.py:70
  90.7 21.3 %collective-permute-start = (s32[1,5]{1,0:T(1,128)S(1)}, s32[1,5]{1,0:T(1,128)S(1)}, u32[]{:S(2)}, u32[]{:S(2)}) collective-permute-start(s32[1,5]{1,0:T(1,128)S(1)} %copy-done.8), channel_id=1, source_target_pairs={{0,1},{1,2},{2,3},{3,4},{4,5},{5,6},{6,7},{7,0},{8,9},{9,10},{10,1... | collective-permute-start | bytes 68 | tf_op jit(solution)/shard_map/ppermute | solution.py:36
  112.0 6.3 %collective-permute-start.1 = (s32[1,5]{1,0:T(1,128)S(1)}, s32[1,5]{1,0:T(1,128)S(1)}, u32[]{:S(2)}, u32[]{:S(2)}) collective-permute-start(s32[1,5]{1,0:T(1,128)S(1)} %collective-permute-done), channel_id=1, source_target_pairs={{0,1},{1,2},{2,3},{3,4},{4,5},{5,6},{6,7},{7,0},{8,9},{9,10},{10,1... | collective-permute-start | bytes 68 | tf_op jit(solution)/shard_map/ppermute | solution.py:36
  118.3 6.3 %collective-permute-start.2 = (s32[1,5]{1,0:T(1,128)S(1)}, s32[1,5]{1,0:T(1,128)S(1)}, u32[]{:S(2)}, u32[]{:S(2)}) collective-permute-start(s32[1,5]{1,0:T(1,128)S(1)} %collective-permute-done.1), channel_id=1, source_target_pairs={{0,1},{1,2},{2,3},{3,4},{4,5},{5,6},{6,7},{7,0},{8,9},{9,10},{10,1... | collective-permute-start | bytes 68 | tf_op jit(solution)/shard_map/ppermute | solution.py:36
  124.5 6.3 %collective-permute-start.3 = (s32[1,5]{1,0:T(1,128)S(1)}, s32[1,5]{1,0:T(1,128)S(1)}, u32[]{:S(2)}, u32[]{:S(2)}) collective-permute-start(s32[1,5]{1,0:T(1,128)S(1)} %collective-permute-done.2), channel_id=1, source_target_pairs={{0,1},{1,2},{2,3},{3,4},{4,5},{5,6},{6,7},{7,0},{8,9},{9,10},{10,1... | collective-permute-start | bytes 68 | tf_op jit(solution)/shard_map/ppermute | solution.py:36
  130.8 6.3 %collective-permute-start.4 = (s32[1,5]{1,0:T(1,128)S(1)}, s32[1,5]{1,0:T(1,128)S(1)}, u32[]{:S(2)}, u32[]{:S(2)}) collective-permute-start(s32[1,5]{1,0:T(1,128)S(1)} %collective-permute-done.3), channel_id=1, source_target_pairs={{0,1},{1,2},{2,3},{3,4},{4,5},{5,6},{6,7},{7,0},{8,9},{9,10},{10,1... | collective-permute-start | bytes 68 | tf_op jit(solution)/shard_map/ppermute | solution.py:36
  137.1 6.3 %collective-permute-start.5 = (s32[1,5]{1,0:T(1,128)S(1)}, s32[1,5]{1,0:T(1,128)S(1)}, u32[]{:S(2)}, u32[]{:S(2)}) collective-permute-start(s32[1,5]{1,0:T(1,128)S(1)} %collective-permute-done.4), channel_id=1, source_target_pairs={{0,1},{1,2},{2,3},{3,4},{4,5},{5,6},{6,7},{7,0},{8,9},{9,10},{10,1... | collective-permute-start | bytes 68 | tf_op jit(solution)/shard_map/ppermute | solution.py:36
  143.3 6.3 %collective-permute-start.6 = (s32[1,5]{1,0:T(1,128)S(1)}, s32[1,5]{1,0:T(1,128)S(1)}, u32[]{:S(2)}, u32[]{:S(2)}) collective-permute-start(s32[1,5]{1,0:T(1,128)S(1)} %collective-permute-done.5), channel_id=1, source_target_pairs={{0,1},{1,2},{2,3},{3,4},{4,5},{5,6},{6,7},{7,0},{8,9},{9,10},{10,1... | collective-permute-start | bytes 68 | tf_op jit(solution)/shard_map/ppermute | solution.py:36
  157.8 6.9 %copy-start.1 = (pred[2048]{0:T(1024)(128)(4,1)S(1)}, pred[2048]{0:T(1024)(128)(4,1)}, u32[]{:S(2)}) copy-start(pred[2048]{0:T(1024)(128)(4,1)} %constant.349) | copy-start | bytes 6148
  157.8 6.9 %copy-start.2 = (pred[2048]{0:T(1024)(128)(4,1)S(1)}, pred[2048]{0:T(1024)(128)(4,1)}, u32[]{:S(2)}) copy-start(pred[2048]{0:T(1024)(128)(4,1)} %constant.350) | copy-start | bytes 6148
  157.8 6.9 %copy-start.3 = (pred[2048]{0:T(1024)(128)(4,1)S(1)}, pred[2048]{0:T(1024)(128)(4,1)}, u32[]{:S(2)}) copy-start(pred[2048]{0:T(1024)(128)(4,1)} %constant.351) | copy-start | bytes 6148
  157.8 6.9 %copy-start.4 = (pred[2048]{0:T(1024)(128)(4,1)S(1)}, pred[2048]{0:T(1024)(128)(4,1)}, u32[]{:S(2)}) copy-start(pred[2048]{0:T(1024)(128)(4,1)} %constant.352) | copy-start | bytes 6148
  157.9 6.9 %copy-start.5 = (pred[2048]{0:T(1024)(128)(4,1)S(1)}, pred[2048]{0:T(1024)(128)(4,1)}, u32[]{:S(2)}) copy-start(pred[2048]{0:T(1024)(128)(4,1)} %constant.353) | copy-start | bytes 6148
  157.9 6.9 %copy-start.6 = (pred[2048]{0:T(1024)(128)(4,1)S(1)}, pred[2048]{0:T(1024)(128)(4,1)}, u32[]{:S(2)}) copy-start(pred[2048]{0:T(1024)(128)(4,1)} %constant.354) | copy-start | bytes 6148
  157.9 6.9 %copy-start.7 = (pred[2048]{0:T(1024)(128)(4,1)S(1)}, pred[2048]{0:T(1024)(128)(4,1)}, u32[]{:S(2)}) copy-start(pred[2048]{0:T(1024)(128)(4,1)} %constant.355) | copy-start | bytes 6148
  173.9 1.9 copy-start
  186.7 1.9 copy-start
  199.6 1.9 copy-start
  212.4 1.9 copy-start
  225.2 1.9 copy-start
  238.0 1.9 copy-start
  250.9 1.9 copy-start
  263.7 1.9 copy-start
Sparse Core Ops, SparseCore 0:
  93.0 59.5 all-gather.1
